TPU v7x, 32 devices: a whole 2x2x4 slice. The times are simulated.
32 devices in a mesh: cell: 8 (over z, y), grp: 4 (over x, core).
Axes of the slice: x: 2, y: 2, z: 4, core: 2. Of those that a mesh axis runs over, the one named last changes fastest.
Arguments:
- initial_guess: float32 [9, 6144], P(None, 'cell'), may hold values from -3 to 3
- right_side: float32 [9, 6144], P(None, 'cell')
- camera_blocks: float32 [9, 9, 6144], P(None, None, 'cell'), as said below
- point_inverse: float32 [3, 3, 16384], P(None, None, ('cell', 'grp')), as said below
- jacobian_tiles: bfloat16 [192, 576, 384], P(('cell', 'grp'))
- tile_pattern: int32 [192, 2], P(('cell', 'grp')), may hold values from 0 to 35, as said below
- cell_load: int32 [8], P('cell'), may hold values from 2 to 6, as said below
Outputs:
- solution: float32 [9, 6144], P(None, 'cell')
- residual: float32 [9, 6144], P(None, 'cell')
Inputs may be any that keep to these rules, and one draw needn't show every extreme that they name: `tile_pattern`: column 0 is below 36, column 1 below 4. `cell_load`: A quarter of the cells, rounded down, chosen from the seed, have 6 live slots on each of their devices; every other cell has 2. Slots at or past the load are unused. `camera_blocks`: each camera block is symmetric with a dominant diagonal. `point_inverse`: each point's block is symmetric with a dominant diagonal.
All inputs are finite; a program needn't handle non-finite values.
Results may differ from a plain program's by a relative error of at most 0.0095.
Values may be sent and summed in bfloat16 or wider, within the bound.
A program may use at most 64 MiB of HBM per device.

v0:
```python
import jax
import jax.numpy as jnp
from jax import lax
from jax.sharding import PartitionSpec as P

CAM_PARAMS = 9
PT_PARAMS = 3
CAM_TILE = 64
PT_TILE = 128
CAM_TILES = 12
PT_TILES = 4
SLOTS = 6
ITERS = 2
HIGHEST = lax.Precision.HIGHEST


def extended(array, sides, width):
    for axis, dim in sides:
        size, length = (lax.axis_size(axis), array.shape[dim])
        up = [(i, (i + 1) % size) for i in range(size)]
        down = [(j, i) for i, j in up]
        last = lax.slice_in_dim(array, length - width, length, axis=dim)
        first = lax.slice_in_dim(array, 0, width, axis=dim)
        before = lax.ppermute(last, axis, up)
        after = lax.ppermute(first, axis, down)
        array = jnp.concatenate([before, array, after], axis=dim)
    return array


def shifted(array, axis, by):
    length = lax.axis_size(axis)
    return lax.ppermute(array, axis, [(i, (i + by) % length) for i in range(length)])


def tile_rows(camera_field, tile_width):
    components = camera_field.shape[0]
    return (
        camera_field.reshape(components, -1, tile_width)
        .transpose(1, 0, 2)
        .reshape(-1, components * tile_width)
    )


def field_columns(row_block, components):
    tile_width = row_block.shape[1] // components
    return row_block.reshape(-1, components, tile_width).transpose(1, 0, 2).reshape(components, -1)


def per_device(
    initial_guess, right_side, camera_blocks, point_inverse, jacobian_tiles, tile_pattern, cell_load
):
    camera_count = initial_guess.shape[1]
    window_ids = tile_pattern[:, 0]
    point_ids = tile_pattern[:, 1]
    live_mask = (lax.iota(jnp.int32, SLOTS) < cell_load[0]).astype(jnp.float32)
    pick_window = window_ids[:, None] == lax.iota(jnp.int32, 3 * CAM_TILES)[None, :]
    pick_point = point_ids[:, None] == lax.iota(jnp.int32, PT_TILES)[None, :]
    diagonal_part = jnp.diagonal(camera_blocks, axis1=0, axis2=1).T
    inverse = point_inverse.reshape(PT_PARAMS, PT_PARAMS, PT_TILES, PT_TILE)
    point_width = PT_PARAMS * PT_TILE

    def apply_schur(direction):
        lowered = direction.astype(jnp.bfloat16)
        window = extended(lowered, (("cell", 1),), camera_count)
        window_rows = tile_rows(window, CAM_TILE)
        chosen = jnp.dot(
            pick_window.astype(jnp.bfloat16), window_rows, preferred_element_type=jnp.float32
        ).astype(jnp.bfloat16)
        forward = (
            jnp.einsum("tk,tkj->tj", chosen, jacobian_tiles, preferred_element_type=jnp.float32)
            * live_mask[:, None]
        )
        point_sums = jnp.dot(pick_point.astype(jnp.float32).T, forward, precision=HIGHEST)
        sectioned = point_sums.reshape(PT_TILES, PT_PARAMS, PT_TILE)
        solved = (
            jnp.einsum("jipq,piq->pjq", inverse, sectioned, precision=HIGHEST)
            .reshape(PT_TILES, point_width)
            .astype(jnp.bfloat16)
        )
        gathered = jnp.dot(
            pick_point.astype(jnp.bfloat16), solved, preferred_element_type=jnp.float32
        ).astype(jnp.bfloat16)
        backward = (
            jnp.einsum("tj,tkj->tk", gathered, jacobian_tiles, preferred_element_type=jnp.float32)
            * live_mask[:, None]
        )
        window_sums = jnp.dot(pick_window.astype(jnp.float32).T, backward, precision=HIGHEST)
        partial_field = field_columns(window_sums, CAM_PARAMS)
        summed = lax.psum(partial_field.astype(jnp.bfloat16), "grp").astype(jnp.float32)
        from_left = shifted(summed[:, 2 * camera_count :], "cell", 1)
        from_right = shifted(summed[:, :camera_count], "cell", -1)
        back_total = summed[:, camera_count : 2 * camera_count] + from_left + from_right
        return jnp.einsum("klc,lc->kc", camera_blocks, direction, precision=HIGHEST) - back_total

    solution = initial_guess
    residual = right_side - apply_schur(solution)
    precond = residual / diagonal_part
    direction = precond
    rz_now = lax.psum(jnp.sum(residual * precond), "cell")
    for iteration in range(ITERS):
        image = apply_schur(direction)
        scaled_image = image / diagonal_part
        curvature_value, cross_term, square = lax.psum(
            (jnp.sum(direction * image), jnp.sum(image * precond), jnp.sum(image * scaled_image)),
            "cell",
        )
        step_size = rz_now / curvature_value
        solution = solution + step_size * direction
        residual = residual - step_size * image
        precond = residual / diagonal_part
        rz_next = rz_now - 2.0 * step_size * cross_term + step_size * step_size * square
        direction = precond + rz_next / rz_now * direction
        rz_now = rz_next
    return (solution, residual)


def solution(mesh):
    placed = (
        P(None, "cell"),
        P(None, "cell"),
        P(None, None, "cell"),
        P(None, None, ("cell", "grp")),
        P(("cell", "grp"), None, None),
        P(("cell", "grp"), None),
        P("cell"),
    )
    return jax.shard_map(
        per_device,
        mesh=mesh,
        in_specs=placed,
        out_specs=(P(None, "cell"), P(None, "cell")),
        check_vma=False,
    )
```

profile of v0, /device:TPU:0, one launch (start us, length us, event | category | flops | bytes accessed | tf_op | source)
XLA Modules:
  0.0 142.2 jit_solution(16594648652979509193)
XLA Ops:
  0.6 1.0 convert_element_type.118
  1.6 6.0 %collective-permute-start.1 = (bf16[9,768]{1,0:T(8,128)(2,1)S(1)}, bf16[9,768]{1,0:T(8,128)(2,1)S(1)}, u32[]{:S(2)}, u32[]{:S(2)}) collective-permute-start(bf16[9,768]{1,0:T(8,128)(2,1)S(1)} %convert_element_type.118), channel_id=1, source_target_pairs={{4,0},{8,4},{12,8},{16,12},{20,16},{24,20},{28,24},{0,28},{5,1},{9... | collective-permute-start | bytes 41480 | tf_op jit(solution)/shard_map/ppermute | solution.py:25
  9.0 1.1 multiply_reduce_fusion.2
  10.9 3.2 %collective-permute-done = bf16[9,768]{1,0:T(8,128)(2,1)S(1)} collective-permute-done((bf16[9,768]{1,0:T(8,128)(2,1)S(1)}, bf16[9,768]{1,0:T(8,128)(2,1)S(1)}, u32[]{:S(2)}, u32[]{:S(2)}) %collective-permute-start) | collective-permute-done | bytes 13856 | tf_op jit(solution)/shard_map/ppermute | solution.py:24
  15.6 0.8 fusion.33
  17.1 10.9 %psum.52 = bf16[9,2304]{1,0:T(8,128)(2,1)S(1)} all-reduce(bf16[9,2304]{1,0:T(8,128)(2,1)S(1)} %convert_element_type.128), channel_id=1, replica_groups=mesh['cell'=8,'grp'=4] {'grp'}, use_global_device_ids=true, to_apply=%region_0.1 | all-reduce | flops 20736 | bytes 82944 | tf_op jit(solution)/shard_map/psum | solution.py:89
  28.7 1.9 %collective-permute-start.3 = (f32[9,768]{1,0:T(8,128)}, f32[9,768]{1,0:T(8,128)S(1)}, u32[]{:S(2)}, u32[]{:S(2)}) collective-permute-start(f32[9,768]{1,0:T(8,128)} %get-tuple-element.21), channel_id=1, source_target_pairs={{0,28},{4,0},{8,4},{12,8},{16,12},{20,16},{24,20},{28,24},{1,29},{... | collective-permute-start | bytes 82952 | tf_op jit(solution)/shard_map/ppermute | solution.py:32
  31.4 1.6 %collective-permute-done.3 = f32[9,768]{1,0:T(8,128)S(1)} collective-permute-done((f32[9,768]{1,0:T(8,128)}, f32[9,768]{1,0:T(8,128)S(1)}, u32[]{:S(2)}, u32[]{:S(2)}) %collective-permute-start.3) | collective-permute-done | bytes 27680 | tf_op jit(solution)/shard_map/ppermute | solution.py:32
  33.6 4.1 %collective-permute-done.2 = f32[9,768]{1,0:T(8,128)} collective-permute-done((f32[9,768]{1,0:T(8,128)}, f32[9,768]{1,0:T(8,128)}, u32[]{:S(2)}, u32[]{:S(2)}) %collective-permute-start.2) | collective-permute-done | bytes 27680 | tf_op jit(solution)/shard_map/ppermute | solution.py:32
  37.7 0.9 fusion.59
  39.1 1.5 %collective-permute-start.4 = (bf16[9,768]{1,0:T(8,128)(2,1)S(1)}, bf16[9,768]{1,0:T(8,128)(2,1)S(1)}, u32[]{:S(2)}, u32[]{:S(2)}) collective-permute-start(bf16[9,768]{1,0:T(8,128)(2,1)S(1)} %get-tuple-element.13), channel_id=1, source_target_pairs={{0,4},{4,8},{8,12},{12,16},{16,20},{20,24},{24,28},{28,0},{1,5},{5... | collective-permute-start | bytes 41480 | tf_op jit(solution)/shard_map/ppermute | solution.py:24
  40.6 1.8 %collective-permute-done.5 = bf16[9,768]{1,0:T(8,128)(2,1)S(1)} collective-permute-done((bf16[9,768]{1,0:T(8,128)(2,1)S(1)}, bf16[9,768]{1,0:T(8,128)(2,1)S(1)}, u32[]{:S(2)}, u32[]{:S(2)}) %collective-permute-start.5) | collective-permute-done | bytes 13856 | tf_op jit(solution)/shard_map/ppermute | solution.py:25
  42.4 3.2 %collective-permute-done.4 = bf16[9,768]{1,0:T(8,128)(2,1)S(1)} collective-permute-done((bf16[9,768]{1,0:T(8,128)(2,1)S(1)}, bf16[9,768]{1,0:T(8,128)(2,1)S(1)}, u32[]{:S(2)}, u32[]{:S(2)}) %collective-permute-start.4) | collective-permute-done | bytes 13856 | tf_op jit(solution)/shard_map/ppermute | solution.py:24
  47.1 0.8 fusion.31
  48.5 10.9 %psum.54 = bf16[9,2304]{1,0:T(8,128)(2,1)S(1)} all-reduce(bf16[9,2304]{1,0:T(8,128)(2,1)S(1)} %convert_element_type.139), channel_id=1, replica_groups=mesh['cell'=8,'grp'=4] {'grp'}, use_global_device_ids=true, to_apply=%region_3.4 | all-reduce | flops 20736 | bytes 82944 | tf_op jit(solution)/shard_map/psum | solution.py:89
  59.6 2.0 %collective-permute-start.6 = (f32[9,768]{1,0:T(8,128)S(1)}, f32[9,768]{1,0:T(8,128)S(1)}, u32[]{:S(2)}, u32[]{:S(2)}) collective-permute-start(f32[9,768]{1,0:T(8,128)S(1)} %get-tuple-element.18), channel_id=1, source_target_pairs={{0,4},{4,8},{8,12},{12,16},{16,20},{20,24},{24,28},{28,0},{1,5},{5... | collective-permute-start | bytes 82952 | tf_op jit(solution)/shard_map/ppermute | solution.py:32
  61.7 2.0 %collective-permute-done.7 = f32[9,768]{1,0:T(8,128)S(1)} collective-permute-done((f32[9,768]{1,0:T(8,128)S(1)}, f32[9,768]{1,0:T(8,128)S(1)}, u32[]{:S(2)}, u32[]{:S(2)}) %collective-permute-start.7) | collective-permute-done | bytes 27680 | tf_op jit(solution)/shard_map/ppermute | solution.py:32
  63.6 2.8 %collective-permute-done.6 = f32[9,768]{1,0:T(8,128)S(1)} collective-permute-done((f32[9,768]{1,0:T(8,128)S(1)}, f32[9,768]{1,0:T(8,128)S(1)}, u32[]{:S(2)}, u32[]{:S(2)}) %collective-permute-start.6) | collective-permute-done | bytes 27680 | tf_op jit(solution)/shard_map/ppermute | solution.py:32
  67.1 17.8 %all-reduce = (f32[]{:T(128)}, f32[]{:T(128)}, f32[]{:T(128)}) all-reduce(f32[]{:T(128)} %get-tuple-element.4, f32[]{:T(128)} %get-tuple-element.3, f32[]{:T(128)} %get-tuple-element.2), channel_id=1, replica_groups=mesh['cell'=8,'grp'=4] {'cell'}, use_global_device_ids=true, to_apply=%region_2.3 | all-reduce | flops 3 | bytes 24 | tf_op jit(solution)/shard_map/psum | solution.py:99
  88.6 2.1 %collective-permute-start.9 = (bf16[9,768]{1,0:T(8,128)(2,1)S(1)}, bf16[9,768]{1,0:T(8,128)(2,1)S(1)}, u32[]{:S(2)}, u32[]{:S(2)}) collective-permute-start(bf16[9,768]{1,0:T(8,128)(2,1)S(1)} %get-tuple-element.10), channel_id=1, source_target_pairs={{4,0},{8,4},{12,8},{16,12},{20,16},{24,20},{28,24},{0,28},{5,1},{9... | collective-permute-start | bytes 41480 | tf_op jit(solution)/shard_map/ppermute | solution.py:25
  90.7 1.8 %collective-permute-done.9 = bf16[9,768]{1,0:T(8,128)(2,1)S(1)} collective-permute-done((bf16[9,768]{1,0:T(8,128)(2,1)S(1)}, bf16[9,768]{1,0:T(8,128)(2,1)S(1)}, u32[]{:S(2)}, u32[]{:S(2)}) %collective-permute-start.9) | collective-permute-done | bytes 13856 | tf_op jit(solution)/shard_map/ppermute | solution.py:25
  92.5 4.7 %collective-permute-done.8 = bf16[9,768]{1,0:T(8,128)(2,1)S(1)} collective-permute-done((bf16[9,768]{1,0:T(8,128)(2,1)S(1)}, bf16[9,768]{1,0:T(8,128)(2,1)S(1)}, u32[]{:S(2)}, u32[]{:S(2)}) %collective-permute-start.8) | collective-permute-done | bytes 13856 | tf_op jit(solution)/shard_map/ppermute | solution.py:24
  97.9 0.9 copy.114
  98.9 0.8 reshape.65
  99.6 1.0 fusion.2
  101.6 0.8 fusion.29
  103.5 1.0 convert_element_type.150
  104.5 10.9 %psum.57 = bf16[9,2304]{1,0:T(8,128)(2,1)S(1)} all-reduce(bf16[9,2304]{1,0:T(8,128)(2,1)S(1)} %convert_element_type.150), channel_id=1, replica_groups=mesh['cell'=8,'grp'=4] {'grp'}, use_global_device_ids=true, to_apply=%region_8.9 | all-reduce | flops 20736 | bytes 82944 | tf_op jit(solution)/shard_map/psum | solution.py:89
  115.6 2.0 %collective-permute-start.10 = (f32[9,768]{1,0:T(8,128)S(1)}, f32[9,768]{1,0:T(8,128)S(1)}, u32[]{:S(2)}, u32[]{:S(2)}) collective-permute-start(f32[9,768]{1,0:T(8,128)S(1)} %get-tuple-element.16), channel_id=1, source_target_pairs={{0,4},{4,8},{8,12},{12,16},{16,20},{20,24},{24,28},{28,0},{1,5},{5... | collective-permute-start | bytes 82952 | tf_op jit(solution)/shard_map/ppermute | solution.py:32
  117.7 2.0 %collective-permute-done.11 = f32[9,768]{1,0:T(8,128)S(1)} collective-permute-done((f32[9,768]{1,0:T(8,128)S(1)}, f32[9,768]{1,0:T(8,128)S(1)}, u32[]{:S(2)}, u32[]{:S(2)}) %collective-permute-start.11) | collective-permute-done | bytes 27680 | tf_op jit(solution)/shard_map/ppermute | solution.py:32
  119.6 2.8 %collective-permute-done.10 = f32[9,768]{1,0:T(8,128)S(1)} collective-permute-done((f32[9,768]{1,0:T(8,128)S(1)}, f32[9,768]{1,0:T(8,128)S(1)}, u32[]{:S(2)}, u32[]{:S(2)}) %collective-permute-start.10) | collective-permute-done | bytes 27680 | tf_op jit(solution)/shard_map/ppermute | solution.py:32
  123.0 17.8 %psum.58 = f32[]{:T(128)} all-reduce(f32[]{:T(128)} %get-tuple-element.8), channel_id=1, replica_groups=mesh['cell'=8,'grp'=4] {'cell'}, use_global_device_ids=true, to_apply=%region_10.11 | all-reduce | flops 1 | bytes 8 | tf_op jit(solution)/shard_map/psum | solution.py:103
  (67 shorter events, 13.5 us)
Async XLA Ops:
  0.6 14.0 %copy-start = (bf16[6,576,384]{2,1,0:T(8,128)(2,1)S(1)}, bf16[6,576,384]{2,1,0:T(8,128)(2,1)}, u32[]{:S(2)}) copy-start(bf16[6,576,384]{2,1,0:T(8,128)(2,1)} %param.11) | copy-start | bytes 7962628
  1.6 9.3 %collective-permute-start.1 = (bf16[9,768]{1,0:T(8,128)(2,1)S(1)}, bf16[9,768]{1,0:T(8,128)(2,1)S(1)}, u32[]{:S(2)}, u32[]{:S(2)}) collective-permute-start(bf16[9,768]{1,0:T(8,128)(2,1)S(1)} %convert_element_type.118), channel_id=1, source_target_pairs={{4,0},{8,4},{12,8},{16,12},{20,16},{24,20},{28,24},{0,28},{5,1},{9... | collective-permute-start | bytes 41480 | tf_op jit(solution)/shard_map/ppermute | solution.py:25
  7.6 6.5 %collective-permute-start = (bf16[9,768]{1,0:T(8,128)(2,1)S(1)}, bf16[9,768]{1,0:T(8,128)(2,1)S(1)}, u32[]{:S(2)}, u32[]{:S(2)}) collective-permute-start(bf16[9,768]{1,0:T(8,128)(2,1)S(1)} %convert_element_type.118), channel_id=1, source_target_pairs={{0,4},{4,8},{8,12},{12,16},{16,20},{20,24},{24,28},{28,0},{1,5},{5... | collective-permute-start | bytes 41480 | tf_op jit(solution)/shard_map/ppermute | solution.py:24
  15.1 15.6 %copy-start.1 = (f32[9,9,768]{2,1,0:T(8,128)S(1)}, f32[9,9,768]{2,1,0:T(8,128)}, u32[]{:S(2)}) copy-start(f32[9,9,768]{2,1,0:T(8,128)} %param.9) | copy-start | bytes 746500
  28.7 4.3 %collective-permute-start.3 = (f32[9,768]{1,0:T(8,128)}, f32[9,768]{1,0:T(8,128)S(1)}, u32[]{:S(2)}, u32[]{:S(2)}) collective-permute-start(f32[9,768]{1,0:T(8,128)} %get-tuple-element.21), channel_id=1, source_target_pairs={{0,28},{4,0},{8,4},{12,8},{16,12},{20,16},{24,20},{28,24},{1,29},{... | collective-permute-start | bytes 82952 | tf_op jit(solution)/shard_map/ppermute | solution.py:32
  30.6 7.1 %collective-permute-start.2 = (f32[9,768]{1,0:T(8,128)}, f32[9,768]{1,0:T(8,128)}, u32[]{:S(2)}, u32[]{:S(2)}) collective-permute-start(f32[9,768]{1,0:T(8,128)} %get-tuple-element.20), channel_id=1, source_target_pairs={{0,4},{4,8},{8,12},{12,16},{16,20},{20,24},{24,28},{28,0},{1,5},{5... | collective-permute-start | bytes 82952 | tf_op jit(solution)/shard_map/ppermute | solution.py:32
  33.0 0.6 copy-start.3
  38.5 3.9 %collective-permute-start.5 = (bf16[9,768]{1,0:T(8,128)(2,1)S(1)}, bf16[9,768]{1,0:T(8,128)(2,1)S(1)}, u32[]{:S(2)}, u32[]{:S(2)}) collective-permute-start(bf16[9,768]{1,0:T(8,128)(2,1)S(1)} %get-tuple-element.13), channel_id=1, source_target_pairs={{4,0},{8,4},{12,8},{16,12},{20,16},{24,20},{28,24},{0,28},{5,1},{9... | collective-permute-start | bytes 41480 | tf_op jit(solution)/shard_map/ppermute | solution.py:25
  39.1 6.5 %collective-permute-start.4 = (bf16[9,768]{1,0:T(8,128)(2,1)S(1)}, bf16[9,768]{1,0:T(8,128)(2,1)S(1)}, u32[]{:S(2)}, u32[]{:S(2)}) collective-permute-start(bf16[9,768]{1,0:T(8,128)(2,1)S(1)} %get-tuple-element.13), channel_id=1, source_target_pairs={{0,4},{4,8},{8,12},{12,16},{16,20},{20,24},{24,28},{28,0},{1,5},{5... | collective-permute-start | bytes 41480 | tf_op jit(solution)/shard_map/ppermute | solution.py:24
  59.5 4.1 %collective-permute-start.7 = (f32[9,768]{1,0:T(8,128)S(1)}, f32[9,768]{1,0:T(8,128)S(1)}, u32[]{:S(2)}, u32[]{:S(2)}) collective-permute-start(f32[9,768]{1,0:T(8,128)S(1)} %get-tuple-element.19), channel_id=1, source_target_pairs={{0,28},{4,0},{8,4},{12,8},{16,12},{20,16},{24,20},{28,24},{1,29},{... | collective-permute-start | bytes 82952 | tf_op jit(solution)/shard_map/ppermute | solution.py:32
  59.6 6.8 %collective-permute-start.6 = (f32[9,768]{1,0:T(8,128)S(1)}, f32[9,768]{1,0:T(8,128)S(1)}, u32[]{:S(2)}, u32[]{:S(2)}) collective-permute-start(f32[9,768]{1,0:T(8,128)S(1)} %get-tuple-element.18), channel_id=1, source_target_pairs={{0,4},{4,8},{8,12},{12,16},{16,20},{20,24},{24,28},{28,0},{1,5},{5... | collective-permute-start | bytes 82952 | tf_op jit(solution)/shard_map/ppermute | solution.py:32
  88.6 3.9 %collective-permute-start.9 = (bf16[9,768]{1,0:T(8,128)(2,1)S(1)}, bf16[9,768]{1,0:T(8,128)(2,1)S(1)}, u32[]{:S(2)}, u32[]{:S(2)}) collective-permute-start(bf16[9,768]{1,0:T(8,128)(2,1)S(1)} %get-tuple-element.10), channel_id=1, source_target_pairs={{4,0},{8,4},{12,8},{16,12},{20,16},{24,20},{28,24},{0,28},{5,1},{9... | collective-permute-start | bytes 41480 | tf_op jit(solution)/shard_map/ppermute | solution.py:25
  90.7 6.5 %collective-permute-start.8 = (bf16[9,768]{1,0:T(8,128)(2,1)S(1)}, bf16[9,768]{1,0:T(8,128)(2,1)S(1)}, u32[]{:S(2)}, u32[]{:S(2)}) collective-permute-start(bf16[9,768]{1,0:T(8,128)(2,1)S(1)} %get-tuple-element.10), channel_id=1, source_target_pairs={{0,4},{4,8},{8,12},{12,16},{16,20},{20,24},{24,28},{28,0},{1,5},{5... | collective-permute-start | bytes 41480 | tf_op jit(solution)/shard_map/ppermute | solution.py:24
  101.1 40.4 %copy-start.2 = (f32[9,768]{1,0:T(8,128)S(1)}, f32[9,768]{1,0:T(8,128)}, u32[]{:S(2)}) copy-start(f32[9,768]{1,0:T(8,128)} %param.7) | copy-start | bytes 82948
  115.5 4.1 %collective-permute-start.11 = (f32[9,768]{1,0:T(8,128)S(1)}, f32[9,768]{1,0:T(8,128)S(1)}, u32[]{:S(2)}, u32[]{:S(2)}) collective-permute-start(f32[9,768]{1,0:T(8,128)S(1)} %get-tuple-element.17), channel_id=1, source_target_pairs={{0,28},{4,0},{8,4},{12,8},{16,12},{20,16},{24,20},{28,24},{1,29},{... | collective-permute-start | bytes 82952 | tf_op jit(solution)/shard_map/ppermute | solution.py:32
  115.6 6.8 %collective-permute-start.10 = (f32[9,768]{1,0:T(8,128)S(1)}, f32[9,768]{1,0:T(8,128)S(1)}, u32[]{:S(2)}, u32[]{:S(2)}) collective-permute-start(f32[9,768]{1,0:T(8,128)S(1)} %get-tuple-element.16), channel_id=1, source_target_pairs={{0,4},{4,8},{8,12},{12,16},{16,20},{20,24},{24,28},{28,0},{1,5},{5... | collective-permute-start | bytes 82952 | tf_op jit(solution)/shard_map/ppermute | solution.py:32
where the time goes:
time: 143 us; the launch traced here: 142 us
  blocking collectives  68.4 us (48%)
  waiting for transfers between devices  29.8 us (21%)
  starting transfers between devices  16.4 us (11%)
  local copies, waits for them, and re-layouts  8.84 us (6%)
  matrix products  7.59 us (5%)
  between operations  5.93 us (4%)
  other arithmetic  5.24 us (4%)
    psum x3, blocking collectives, apply_schur(): lax.psum(partial_field.astype(jnp.bfloat16), 'grp').astype(jnp.float32)  32.8 us
    psum x1, blocking collectives, per_device(): lax.psum((jnp.sum(direction * image), jnp.sum(image * precond), jnp.sum(i...  17.8 us
    psum x1, blocking collectives, per_device(): rz_now = lax.psum(jnp.sum(residual * precond), 'cell')  17.8 us
    ppermute x6, waiting for transfers between devices, shifted(): lax.ppermute(array, axis, [(i, (i + by) % length) for i in range(length)])  15.1 us
    ppermute x3, waiting for transfers between devices, extended(): before = lax.ppermute(last, axis, up)  11.1 us
    ppermute x3, starting transfers between devices, extended(): after = lax.ppermute(first, axis, down)  8.66 us
    ppermute x6, starting transfers between devices, shifted(): lax.ppermute(array, axis, [(i, (i + by) % length) for i in range(length)])  6.17 us
    ppermute x3, waiting for transfers between devices, extended(): after = lax.ppermute(first, axis, down)  3.56 us
  transfers between devices with their start and end apart: 12, of which 11 were waited for; matrix products, arithmetic and copies ran while one was open for 2% of the time, Pallas kernels for 0%

commit v1 on v0

--- a/solution.py
+++ b/solution.py
@@ -86,7 +86,9 @@
         )
         window_sums = jnp.dot(pick_window.astype(jnp.float32).T, backward, precision=HIGHEST)
         partial_field = field_columns(window_sums, CAM_PARAMS)
-        summed = lax.psum(partial_field.astype(jnp.bfloat16), "grp").astype(jnp.float32)
+        summed = jnp.sum(lax.all_gather(partial_field.astype(jnp.bfloat16), "grp"), axis=0).astype(
+            jnp.float32
+        )
         from_left = shifted(summed[:, 2 * camera_count :], "cell", 1)
         from_right = shifted(summed[:, :camera_count], "cell", -1)
         back_total = summed[:, camera_count : 2 * camera_count] + from_left + from_right

time: 143 us -> 130 us (0.909)
  blocking collectives: 68.4 us -> 54.1 us
  other arithmetic: 5.24 us -> 10.5 us
  waiting for transfers between devices: 29.8 us -> 27.6 us
    psum x3 -> x0, blocking collectives: 32.8 us -> none  [apply_schur(): lax.psum(partial_field.astype(jnp.bfloat16), 'grp').astype(jnp.float32)]
    all_gather x0 -> x3, blocking collectives: none -> 18.3 us  [apply_schur(): lax.all_gather(partial_field.astype(jnp.bfloat16), 'grp')]
    convert_element_type x3, other arithmetic: 0.04 us -> 1.81 us  [apply_schur(): jnp.sum(lax.all_gather(partial_field.astype(jnp.bfloat16), 'grp'), axis=0)]
    slice x3, local copies, waits for them, and re-layouts: 0.66 us -> 2.18 us  [apply_schur(): from_left = shifted(summed[:, 2 * camera_count:], 'cell', 1)]
    reshape x6, local copies, waits for them, and re-layouts: 1.94 us -> 0.43 us  [tile_rows(): camera_field.reshape(components, -1, tile_width).transpose(1, 0, 2)]
  transfers between devices with their start and end apart: 12 -> 12, of which waited for: 11 -> 11; matrix products, arithmetic and copies ran while one was open for 2% -> 5% of each run, Pallas kernels for 0% -> 0%
where the time goes in v1:
time: 130 us; the launch traced here: 129 us
  blocking collectives  54.1 us (42%)
  waiting for transfers between devices  27.6 us (21%)
  starting transfers between devices  16.4 us (13%)
  other arithmetic  10.5 us (8%)
  local copies, waits for them, and re-layouts  7.97 us (6%)
  matrix products  6.79 us (5%)
  between operations  6.1 us (5%)
    all_gather x3, blocking collectives, apply_schur(): lax.all_gather(partial_field.astype(jnp.bfloat16), 'grp')  18.3 us
    psum x1, blocking collectives, per_device(): rz_now = lax.psum(jnp.sum(residual * precond), 'cell')  17.9 us
    psum x1, blocking collectives, per_device(): lax.psum((jnp.sum(direction * image), jnp.sum(image * precond), jnp.sum(i...  17.9 us
    ppermute x6, waiting for transfers between devices, shifted(): lax.ppermute(array, axis, [(i, (i + by) % length) for i in range(length)])  14.1 us
    ppermute x3, waiting for transfers between devices, extended(): before = lax.ppermute(last, axis, up)  9.97 us
    ppermute x3, starting transfers between devices, extended(): after = lax.ppermute(first, axis, down)  7.98 us
    ppermute x6, starting transfers between devices, shifted(): lax.ppermute(array, axis, [(i, (i + by) % length) for i in range(length)])  6.25 us
    ppermute x3, waiting for transfers between devices, extended(): after = lax.ppermute(first, axis, down)  3.6 us
  transfers between devices with their start and end apart: 12, of which 11 were waited for; matrix products, arithmetic and copies ran while one was open for 5% of the time, Pallas kernels for 0%

profile of v1, /device:TPU:0, one launch (start us, length us, event | category | flops | bytes accessed | tf_op | source)
XLA Modules:
  0.0 129.4 jit_solution(2834894292146309394)
XLA Ops:
  0.6 1.0 convert_element_type.145
  1.6 6.0 %collective-permute-start.1 = (bf16[9,768]{1,0:T(8,128)(2,1)S(1)}, bf16[9,768]{1,0:T(8,128)(2,1)S(1)}, u32[]{:S(2)}, u32[]{:S(2)}) collective-permute-start(bf16[9,768]{1,0:T(8,128)(2,1)S(1)} %convert_element_type.145), channel_id=1, source_target_pairs={{4,0},{8,4},{12,8},{16,12},{20,16},{24,20},{28,24},{0,28},{5,1},{9... | collective-permute-start | bytes 41480 | tf_op jit(solution)/shard_map/ppermute | solution.py:25
  9.0 1.7 %multiply_reduce_fusion.2 = f32[768,9]{0,1:T(8,128)} fusion(f32[9,9,768]{2,1,0:T(8,128)} %param.9, f32[768,9]{0,1:T(8,128)} %bitcast.120), kind=kLoop, calls=%fused_computation.21 | loop fusion | flops 117504 | bytes 304128 | tf_op jit(solution)/shard_map/klc,lc->kc/dot_general | solution.py:95
  11.5 2.6 %collective-permute-done = bf16[9,768]{1,0:T(8,128)(2,1)S(1)} collective-permute-done((bf16[9,768]{1,0:T(8,128)(2,1)S(1)}, bf16[9,768]{1,0:T(8,128)(2,1)S(1)}, u32[]{:S(2)}, u32[]{:S(2)}) %collective-permute-start) | collective-permute-done | bytes 13856 | tf_op jit(solution)/shard_map/ppermute | solution.py:24
  15.6 0.8 fusion.33
  17.7 6.1 %all_gather.12 = bf16[4,9,2304]{2,1,0:T(8,128)(2,1)S(1)} all-gather(bf16[1,9,2304]{2,1,0:T(8,128)(2,1)} %convert_element_type.155), channel_id=1, replica_groups=mesh['cell'=8,'grp'=4] {'grp'}, dimensions={0}, use_global_device_ids=true | all-gather | bytes 207360 | tf_op jit(solution)/shard_map/all_gather | solution.py:89
  24.5 2.1 %collective-permute-start.3 = (f32[9,768]{1,0:T(8,128)}, f32[9,768]{1,0:T(8,128)S(1)}, u32[]{:S(2)}, u32[]{:S(2)}) collective-permute-start(f32[9,768]{1,0:T(8,128)} %get-tuple-element.21), channel_id=1, source_target_pairs={{0,28},{4,0},{8,4},{12,8},{16,12},{20,16},{24,20},{28,24},{1,29},{... | collective-permute-start | bytes 82952 | tf_op jit(solution)/shard_map/ppermute | solution.py:32
  27.3 1.5 %collective-permute-done.3 = f32[9,768]{1,0:T(8,128)S(1)} collective-permute-done((f32[9,768]{1,0:T(8,128)}, f32[9,768]{1,0:T(8,128)S(1)}, u32[]{:S(2)}, u32[]{:S(2)}) %collective-permute-start.3) | collective-permute-done | bytes 27680 | tf_op jit(solution)/shard_map/ppermute | solution.py:32
  28.8 4.9 %collective-permute-done.2 = f32[9,768]{1,0:T(8,128)} collective-permute-done((f32[9,768]{1,0:T(8,128)}, f32[9,768]{1,0:T(8,128)}, u32[]{:S(2)}, u32[]{:S(2)}) %collective-permute-start.2) | collective-permute-done | bytes 27680 | tf_op jit(solution)/shard_map/ppermute | solution.py:32
  33.7 0.9 fusion.59
  34.7 2.0 %collective-permute-start.4 = (bf16[9,768]{1,0:T(8,128)(2,1)S(1)}, bf16[9,768]{1,0:T(8,128)(2,1)S(1)}, u32[]{:S(2)}, u32[]{:S(2)}) collective-permute-start(bf16[9,768]{1,0:T(8,128)(2,1)S(1)} %get-tuple-element.13), channel_id=1, source_target_pairs={{0,4},{4,8},{8,12},{12,16},{16,20},{20,24},{24,28},{28,0},{1,5},{5... | collective-permute-start | bytes 41480 | tf_op jit(solution)/shard_map/ppermute | solution.py:24
  36.7 1.8 %collective-permute-done.5 = bf16[9,768]{1,0:T(8,128)(2,1)S(1)} collective-permute-done((bf16[9,768]{1,0:T(8,128)(2,1)S(1)}, bf16[9,768]{1,0:T(8,128)(2,1)S(1)}, u32[]{:S(2)}, u32[]{:S(2)}) %collective-permute-start.5) | collective-permute-done | bytes 13856 | tf_op jit(solution)/shard_map/ppermute | solution.py:25
  38.5 2.8 %collective-permute-done.4 = bf16[9,768]{1,0:T(8,128)(2,1)S(1)} collective-permute-done((bf16[9,768]{1,0:T(8,128)(2,1)S(1)}, bf16[9,768]{1,0:T(8,128)(2,1)S(1)}, u32[]{:S(2)}, u32[]{:S(2)}) %collective-permute-start.4) | collective-permute-done | bytes 13856 | tf_op jit(solution)/shard_map/ppermute | solution.py:24
  42.7 0.8 fusion.31
  44.8 6.1 %all_gather.13 = bf16[4,9,2304]{2,1,0:T(8,128)(2,1)S(1)} all-gather(bf16[1,9,2304]{2,1,0:T(8,128)(2,1)} %convert_element_type.166), channel_id=1, replica_groups=mesh['cell'=8,'grp'=4] {'grp'}, dimensions={0}, use_global_device_ids=true | all-gather | bytes 207360 | tf_op jit(solution)/shard_map/all_gather | solution.py:89
  51.5 0.8 fusion.62
  52.4 2.0 %collective-permute-start.6 = (f32[9,768]{1,0:T(8,128)S(1)}, f32[9,768]{1,0:T(8,128)S(1)}, u32[]{:S(2)}, u32[]{:S(2)}) collective-permute-start(f32[9,768]{1,0:T(8,128)S(1)} %get-tuple-element.18), channel_id=1, source_target_pairs={{0,4},{4,8},{8,12},{12,16},{16,20},{20,24},{24,28},{28,0},{1,5},{5... | collective-permute-start | bytes 82952 | tf_op jit(solution)/shard_map/ppermute | solution.py:32
  54.5 0.9 convert_element_type.167
  55.4 1.1 collective-permute-done.7
  56.4 2.8 %collective-permute-done.6 = f32[9,768]{1,0:T(8,128)S(1)} collective-permute-done((f32[9,768]{1,0:T(8,128)S(1)}, f32[9,768]{1,0:T(8,128)S(1)}, u32[]{:S(2)}, u32[]{:S(2)}) %collective-permute-start.6) | collective-permute-done | bytes 27680 | tf_op jit(solution)/shard_map/ppermute | solution.py:32
  59.9 17.9 %all-reduce = (f32[]{:T(128)}, f32[]{:T(128)}, f32[]{:T(128)}) all-reduce(f32[]{:T(128)} %get-tuple-element.4, f32[]{:T(128)} %get-tuple-element.3, f32[]{:T(128)} %get-tuple-element.2), channel_id=1, replica_groups=mesh['cell'=8,'grp'=4] {'cell'}, use_global_device_ids=true, to_apply=%region_2.3 | all-reduce | flops 3 | bytes 24 | tf_op jit(solution)/shard_map/psum | solution.py:101
  82.4 1.9 %collective-permute-start.9 = (bf16[9,768]{1,0:T(8,128)(2,1)S(1)}, bf16[9,768]{1,0:T(8,128)(2,1)S(1)}, u32[]{:S(2)}, u32[]{:S(2)}) collective-permute-start(bf16[9,768]{1,0:T(8,128)(2,1)S(1)} %get-tuple-element.10), channel_id=1, source_target_pairs={{4,0},{8,4},{12,8},{16,12},{20,16},{24,20},{28,24},{0,28},{5,1},{9... | collective-permute-start | bytes 41480 | tf_op jit(solution)/shard_map/ppermute | solution.py:25
  84.4 1.8 %collective-permute-done.9 = bf16[9,768]{1,0:T(8,128)(2,1)S(1)} collective-permute-done((bf16[9,768]{1,0:T(8,128)(2,1)S(1)}, bf16[9,768]{1,0:T(8,128)(2,1)S(1)}, u32[]{:S(2)}, u32[]{:S(2)}) %collective-permute-start.9) | collective-permute-done | bytes 13856 | tf_op jit(solution)/shard_map/ppermute | solution.py:25
  86.2 4.6 %collective-permute-done.8 = bf16[9,768]{1,0:T(8,128)(2,1)S(1)} collective-permute-done((bf16[9,768]{1,0:T(8,128)(2,1)S(1)}, bf16[9,768]{1,0:T(8,128)(2,1)S(1)}, u32[]{:S(2)}, u32[]{:S(2)}) %collective-permute-start.8) | collective-permute-done | bytes 13856 | tf_op jit(solution)/shard_map/ppermute | solution.py:24
  92.3 0.8 fusion.29
  94.3 6.1 %all_gather.14 = bf16[4,9,2304]{2,1,0:T(8,128)(2,1)S(1)} all-gather(bf16[1,9,2304]{2,1,0:T(8,128)(2,1)} %convert_element_type.177), channel_id=1, replica_groups=mesh['cell'=8,'grp'=4] {'grp'}, dimensions={0}, use_global_device_ids=true | all-gather | bytes 207360 | tf_op jit(solution)/shard_map/all_gather | solution.py:89
  101.9 2.0 %collective-permute-start.10 = (f32[9,768]{1,0:T(8,128)S(1)}, f32[9,768]{1,0:T(8,128)S(1)}, u32[]{:S(2)}, u32[]{:S(2)}) collective-permute-start(f32[9,768]{1,0:T(8,128)S(1)} %get-tuple-element.16), channel_id=1, source_target_pairs={{0,4},{4,8},{8,12},{12,16},{16,20},{20,24},{24,28},{28,0},{1,5},{5... | collective-permute-start | bytes 82952 | tf_op jit(solution)/shard_map/ppermute | solution.py:32
  104.0 0.9 convert_element_type.178
  104.9 1.1 collective-permute-done.11
  106.0 2.8 %collective-permute-done.10 = f32[9,768]{1,0:T(8,128)S(1)} collective-permute-done((f32[9,768]{1,0:T(8,128)S(1)}, f32[9,768]{1,0:T(8,128)S(1)}, u32[]{:S(2)}, u32[]{:S(2)}) %collective-permute-start.10) | collective-permute-done | bytes 27680 | tf_op jit(solution)/shard_map/ppermute | solution.py:32
  109.4 17.9 %psum.34 = f32[]{:T(128)} all-reduce(f32[]{:T(128)} %get-tuple-element.8), channel_id=1, replica_groups=mesh['cell'=8,'grp'=4] {'cell'}, use_global_device_ids=true, to_apply=%region_10.11 | all-reduce | flops 1 | bytes 8 | tf_op jit(solution)/shard_map/psum | solution.py:105
  127.9 1.5 %multiply_subtract_fusion = (f32[9,768]{1,0:T(8,128)}, f32[9,768]{1,0:T(8,128)}) fusion(f32[9,768]{1,0:T(8,128)S(1)} %get-tuple-element.9, f32[]{:T(128)S(6)} %div.23, f32[9,768]{1,0:T(8,128)S(1)} %get-tuple-element.15, f32[9,768]{1,0:T(8,128)} %copy-done.3, f32[]{:T(128)S(6)} %div.19, f32[9,768]{1,0:T(8,128)S(1)} %copy-done.2, f32[9,768]{1,0:T(8,128)} %param.7, ...), kind=kLoop, calls=%fused_computation.39 | loop fusion | flops 55296 | bytes 221192 | tf_op jit(solution)/shard_map/sub | solution.py:111
  (74 shorter events, 15.5 us)
Async XLA Ops:
  0.6 14.0 %copy-start = (bf16[6,576,384]{2,1,0:T(8,128)(2,1)S(1)}, bf16[6,576,384]{2,1,0:T(8,128)(2,1)}, u32[]{:S(2)}) copy-start(bf16[6,576,384]{2,1,0:T(8,128)(2,1)} %param.11) | copy-start | bytes 7962628
  1.6 9.9 %collective-permute-start.1 = (bf16[9,768]{1,0:T(8,128)(2,1)S(1)}, bf16[9,768]{1,0:T(8,128)(2,1)S(1)}, u32[]{:S(2)}, u32[]{:S(2)}) collective-permute-start(bf16[9,768]{1,0:T(8,128)(2,1)S(1)} %convert_element_type.145), channel_id=1, source_target_pairs={{4,0},{8,4},{12,8},{16,12},{20,16},{24,20},{28,24},{0,28},{5,1},{9... | collective-permute-start | bytes 41480 | tf_op jit(solution)/shard_map/ppermute | solution.py:25
  7.6 6.5 %collective-permute-start = (bf16[9,768]{1,0:T(8,128)(2,1)S(1)}, bf16[9,768]{1,0:T(8,128)(2,1)S(1)}, u32[]{:S(2)}, u32[]{:S(2)}) collective-permute-start(bf16[9,768]{1,0:T(8,128)(2,1)S(1)} %convert_element_type.145), channel_id=1, source_target_pairs={{0,4},{4,8},{8,12},{12,16},{16,20},{20,24},{24,28},{28,0},{1,5},{5... | collective-permute-start | bytes 41480 | tf_op jit(solution)/shard_map/ppermute | solution.py:24
  11.5 31.0 %copy-start.4 = (f32[3,3,4,128]{3,2,1,0:T(4,128)}, f32[3,3,4,128]{3,2,1,0:T(4,128)S(1)}, u32[]{:S(2)}) copy-start(f32[3,3,4,128]{3,2,1,0:T(4,128)S(1)} %reshape.90) | copy-start | bytes 55300
  15.1 11.5 %copy-start.1 = (f32[9,9,768]{2,1,0:T(8,128)S(1)}, f32[9,9,768]{2,1,0:T(8,128)}, u32[]{:S(2)}) copy-start(f32[9,9,768]{2,1,0:T(8,128)} %param.9) | copy-start | bytes 746500
  24.5 4.3 %collective-permute-start.3 = (f32[9,768]{1,0:T(8,128)}, f32[9,768]{1,0:T(8,128)S(1)}, u32[]{:S(2)}, u32[]{:S(2)}) collective-permute-start(f32[9,768]{1,0:T(8,128)} %get-tuple-element.21), channel_id=1, source_target_pairs={{0,28},{4,0},{8,4},{12,8},{16,12},{20,16},{24,20},{28,24},{1,29},{... | collective-permute-start | bytes 82952 | tf_op jit(solution)/shard_map/ppermute | solution.py:32
  26.6 7.1 %collective-permute-start.2 = (f32[9,768]{1,0:T(8,128)}, f32[9,768]{1,0:T(8,128)}, u32[]{:S(2)}, u32[]{:S(2)}) collective-permute-start(f32[9,768]{1,0:T(8,128)} %get-tuple-element.20), channel_id=1, source_target_pairs={{0,4},{4,8},{8,12},{12,16},{16,20},{20,24},{24,28},{28,0},{1,5},{5... | collective-permute-start | bytes 82952 | tf_op jit(solution)/shard_map/ppermute | solution.py:32
  34.6 3.9 %collective-permute-start.5 = (bf16[9,768]{1,0:T(8,128)(2,1)S(1)}, bf16[9,768]{1,0:T(8,128)(2,1)S(1)}, u32[]{:S(2)}, u32[]{:S(2)}) collective-permute-start(bf16[9,768]{1,0:T(8,128)(2,1)S(1)} %get-tuple-element.13), channel_id=1, source_target_pairs={{4,0},{8,4},{12,8},{16,12},{20,16},{24,20},{28,24},{0,28},{5,1},{9... | collective-permute-start | bytes 41480 | tf_op jit(solution)/shard_map/ppermute | solution.py:25
  34.7 6.6 %collective-permute-start.4 = (bf16[9,768]{1,0:T(8,128)(2,1)S(1)}, bf16[9,768]{1,0:T(8,128)(2,1)S(1)}, u32[]{:S(2)}, u32[]{:S(2)}) collective-permute-start(bf16[9,768]{1,0:T(8,128)(2,1)S(1)} %get-tuple-element.13), channel_id=1, source_target_pairs={{0,4},{4,8},{8,12},{12,16},{16,20},{20,24},{24,28},{28,0},{1,5},{5... | collective-permute-start | bytes 41480 | tf_op jit(solution)/shard_map/ppermute | solution.py:24
  51.5 40.5 %copy-start.5 = (f32[3,3,4,128]{3,2,1,0:T(4,128)S(1)}, f32[3,3,4,128]{3,2,1,0:T(4,128)}, u32[]{:S(2)}) copy-start(f32[3,3,4,128]{3,2,1,0:T(4,128)} %copy-done.4) | copy-start | bytes 55300
  52.3 4.1 %collective-permute-start.7 = (f32[9,768]{1,0:T(8,128)S(1)}, f32[9,768]{1,0:T(8,128)S(1)}, u32[]{:S(2)}, u32[]{:S(2)}) collective-permute-start(f32[9,768]{1,0:T(8,128)S(1)} %get-tuple-element.19), channel_id=1, source_target_pairs={{0,28},{4,0},{8,4},{12,8},{16,12},{20,16},{24,20},{28,24},{1,29},{... | collective-permute-start | bytes 82952 | tf_op jit(solution)/shard_map/ppermute | solution.py:32
  52.4 6.8 %collective-permute-start.6 = (f32[9,768]{1,0:T(8,128)S(1)}, f32[9,768]{1,0:T(8,128)S(1)}, u32[]{:S(2)}, u32[]{:S(2)}) collective-permute-start(f32[9,768]{1,0:T(8,128)S(1)} %get-tuple-element.18), channel_id=1, source_target_pairs={{0,4},{4,8},{8,12},{12,16},{16,20},{20,24},{24,28},{28,0},{1,5},{5... | collective-permute-start | bytes 82952 | tf_op jit(solution)/shard_map/ppermute | solution.py:32
  59.9 30.9 %copy-start.3 = (f32[9,768]{1,0:T(8,128)}, f32[9,768]{1,0:T(8,128)S(1)}, u32[]{:S(2)}) copy-start(f32[9,768]{1,0:T(8,128)S(1)} %get-tuple-element.12) | copy-start | bytes 82948
  82.4 3.8 %collective-permute-start.9 = (bf16[9,768]{1,0:T(8,128)(2,1)S(1)}, bf16[9,768]{1,0:T(8,128)(2,1)S(1)}, u32[]{:S(2)}, u32[]{:S(2)}) collective-permute-start(bf16[9,768]{1,0:T(8,128)(2,1)S(1)} %get-tuple-element.10), channel_id=1, source_target_pairs={{4,0},{8,4},{12,8},{16,12},{20,16},{24,20},{28,24},{0,28},{5,1},{9... | collective-permute-start | bytes 41480 | tf_op jit(solution)/shard_map/ppermute | solution.py:25
  84.3 6.5 %collective-permute-start.8 = (bf16[9,768]{1,0:T(8,128)(2,1)S(1)}, bf16[9,768]{1,0:T(8,128)(2,1)S(1)}, u32[]{:S(2)}, u32[]{:S(2)}) collective-permute-start(bf16[9,768]{1,0:T(8,128)(2,1)S(1)} %get-tuple-element.10), channel_id=1, source_target_pairs={{0,4},{4,8},{8,12},{12,16},{16,20},{20,24},{24,28},{28,0},{1,5},{5... | collective-permute-start | bytes 41480 | tf_op jit(solution)/shard_map/ppermute | solution.py:24
  91.8 12.1 %copy-start.2 = (f32[9,768]{1,0:T(8,128)S(1)}, f32[9,768]{1,0:T(8,128)}, u32[]{:S(2)}) copy-start(f32[9,768]{1,0:T(8,128)} %get-tuple-element.11) | copy-start | bytes 82948
  101.8 4.1 %collective-permute-start.11 = (f32[9,768]{1,0:T(8,128)S(1)}, f32[9,768]{1,0:T(8,128)S(1)}, u32[]{:S(2)}, u32[]{:S(2)}) collective-permute-start(f32[9,768]{1,0:T(8,128)S(1)} %get-tuple-element.17), channel_id=1, source_target_pairs={{0,28},{4,0},{8,4},{12,8},{16,12},{20,16},{24,20},{28,24},{1,29},{... | collective-permute-start | bytes 82952 | tf_op jit(solution)/shard_map/ppermute | solution.py:32
  101.9 6.8 %collective-permute-start.10 = (f32[9,768]{1,0:T(8,128)S(1)}, f32[9,768]{1,0:T(8,128)S(1)}, u32[]{:S(2)}, u32[]{:S(2)}) collective-permute-start(f32[9,768]{1,0:T(8,128)S(1)} %get-tuple-element.16), channel_id=1, source_target_pairs={{0,4},{4,8},{8,12},{12,16},{16,20},{20,24},{24,28},{28,0},{1,5},{5... | collective-permute-start | bytes 82952 | tf_op jit(solution)/shard_map/ppermute | solution.py:32
